TPU v7x, 32 devices: a whole 2x2x4 slice. The times are simulated.
32 devices in a mesh: box: 8 (over z, y), face: 4 (over x, core).
Axes of the slice: x: 2, y: 2, z: 4, core: 2. Of those that a mesh axis runs over, the one named last changes fastest.
Arguments:
- blocks: bfloat16 [32, 24, 24, 128, 128], P('box', 'face'), may hold values from -1 to 2
- pattern: int32 [32, 24, 24], P('box', 'face'), may hold values from 0 to 1, as said below
- shared: int32 [32, 4], P('box'), may hold values from 0 to 23, as said below
- sketch: bfloat16 [3072, 256], replicated, may hold values from -6 to 6
Outputs:
- merged: bfloat16 [32, 3072, 256], P('box', 'face')
Inputs may be any that keep to these rules, and one draw needn't show every extreme that they name: `pattern`: 1 where a block is stored; every diagonal block is stored. `shared`: 4 distinct block indices in increasing order.
All inputs are finite; a program needn't handle non-finite values.
Results may differ from a plain program's by a relative error of at most 0.0085.
Values may be sent and summed in bfloat16 or wider, within the bound.
No kernel may reach another device: no remote copies, remote signals or barrier semaphores. Data moves between devices by JAX's collectives and lax.ppermute only.
A program may use at most 128 MiB of HBM per device.

v0:
```python
import jax
import jax.numpy as jnp
from jax import lax
from jax.sharding import PartitionSpec as P

ITERS = 4


def partner(value, axis, stride):
    mask = 2**stride
    pairs = [(source, source ^ mask) for source in range(lax.axis_size(axis))]
    return lax.ppermute(value, axis, pairs)


def local(blocks, pattern, shared, sketch):
    box_count, row_blocks, all_blocks, blk_size, _ = blocks.shape
    col_count = sketch.shape[1]
    row_start = lax.axis_index("face") * row_blocks
    block_ids = lax.iota(jnp.int32, all_blocks)
    rows_here = row_start + lax.iota(jnp.int32, row_blocks)
    chosen = shared[:, :, None] == block_ids[None, None, :]
    exterior = 1 - jnp.any(chosen, axis=1).astype(jnp.int32)
    keep_ext = (pattern * exterior[:, None, :]).astype(blocks.dtype)
    kept_ext = blocks * keep_ext[:, :, :, None, None]
    sketch_blocks = sketch.reshape(all_blocks, blk_size, col_count)
    sketched = jnp.einsum(
        "brjpq,jqc->brpc", kept_ext, sketch_blocks, preferred_element_type=jnp.float32
    ).astype(jnp.bfloat16)
    column_pick = chosen.astype(jnp.bfloat16)
    side_cols = jnp.einsum(
        "brjpq,bkj->brkpq", blocks, column_pick, preferred_element_type=jnp.float32
    )
    side_mask = jnp.einsum(
        "brj,bkj->brk",
        pattern.astype(jnp.float32),
        chosen.astype(jnp.float32),
        precision=lax.Precision.HIGHEST,
    )
    side_cols = (side_cols * side_mask[:, :, :, None, None]).astype(jnp.bfloat16)
    row_pick_b16 = (shared[:, :, None] == rows_here[None, None, :]).astype(jnp.bfloat16)
    slot_y = jnp.einsum(
        "bkr,brpc->bkpc", row_pick_b16, sketched, preferred_element_type=jnp.float32
    )
    slot_side = jnp.einsum(
        "bkr,brlpq->bklpq", row_pick_b16, side_cols, preferred_element_type=jnp.float32
    )
    here_y, here_side = (
        lax.psum(slot_y.astype(jnp.bfloat16), "face").astype(jnp.float32),
        lax.psum(slot_side.astype(jnp.bfloat16), "face").astype(jnp.float32),
    )
    there_y, there_side = partner(
        (here_y.astype(jnp.bfloat16), here_side.astype(jnp.bfloat16)), "box", 0
    )
    right_side = here_y + there_y.astype(jnp.float32)
    system = here_side + there_side.astype(jnp.float32)
    diag_sum = jnp.diagonal(jnp.diagonal(system, axis1=1, axis2=2), axis1=1, axis2=2)
    part_cols = col_count // lax.axis_size("face")
    col_start = lax.axis_index("face") * part_cols
    part_rhs = lax.dynamic_slice_in_dim(right_side, col_start, part_cols, 3)
    potential = part_rhs / diag_sum[..., None]
    for sweep_index in range(ITERS - 1):
        applied = jnp.einsum("bklpq,blqc->bkpc", system, potential, precision=lax.Precision.HIGHEST)
        potential = potential + (part_rhs - applied) / diag_sum[..., None]
    potential = lax.all_gather(potential.astype(jnp.bfloat16), "face", axis=3, tiled=True).astype(
        potential.dtype
    )
    correction = jnp.einsum(
        "brkpq,bkqc->brpc",
        side_cols,
        potential.astype(jnp.bfloat16),
        preferred_element_type=jnp.float32,
    )
    merged = (sketched.astype(jnp.float32) - correction).astype(jnp.bfloat16)
    return merged.reshape(box_count, row_blocks * blk_size, col_count)


def solution(mesh):
    return jax.shard_map(
        local,
        mesh=mesh,
        in_specs=(P("box", "face", None, None, None), P("box", "face", None), P("box", None), P()),
        out_specs=P("box", "face", None),
        check_vma=False,
    )
```

profile of v0, /device:TPU:0, one launch (start us, length us, event | category | flops | bytes accessed | tf_op | source)
XLA Modules:
  0.0 247.8 jit_solution(17600785656989528693)
XLA Ops:
  6.5 0.0 copy-start
  6.5 0.0 all-reduce.3.cloned.1.call-start
  6.5 0.9 fusion.40
  7.4 0.8 fusion.49
  8.2 0.9 convolution_bitcast_fusion
  9.1 0.1 copy.62
  9.2 0.0 copy-start.5
  9.2 25.3 %fusion = f32[4,4,6,128,128]{4,1,3,2,0:T(4,128)} fusion(bf16[4,6,24,128,128]{4,3,2,1,0:T(8,128)(2,1)} %param.4, s32[4,4]{1,0:T(4,128)} %param.6), kind=kOutput, calls=%fused_computation.2 | convolution fusion | flops 75497856 | bytes 25165888 | tf_op jit(solution)/shard_map/brjpq,bkj->brkpq/dot_general | solution.py:30
  34.5 0.0 copy-start.2
  34.5 3.8 %fusion.5 = bf16[4,6,4,128,128]{4,3,2,1,0:T(8,128)(2,1)S(1)} fusion(f32[4,4,6,128,128]{4,1,3,2,0:T(4,128)} %fusion, f32[4,6,4]{2,1,0:T(8,128)S(1)} %copy.62), kind=kLoop, calls=%fused_computation.8 | loop fusion | flops 3145728 | bytes 9437568 | tf_op jit(solution)/shard_map/convert_element_type | solution.py:39
  38.3 0.0 copy-done.5
  38.3 0.0 copy-start.3
  38.3 2.3 fusion.6
  40.6 0.0 copy-done.3
  40.6 1.9 copy.98
  42.5 0.0 copy-done
  42.5 2.1 copy-done.2
  44.6 5.5 %bitcast_convert_fusion = bf16[4,6,128,256]{3,2,1,0:T(8,128)(2,1)S(1)} fusion(bf16[24,128,256,1,1]{2,1,0,4,3:T(8,128)(2,1)S(1)} %bitcast.90, bf16[4,6,24,128,128]{4,3,2,1,0:T(8,128)(2,1)S(1)} %copy-done.2, bf16[4,6,24]{2,1,0:T(8,128)(2,1)S(1)} %copy.58), kind=kOutput, calls=%fused_computation.19 | convolution fusion | flops 4842061824 | bytes 22021248 | tf_op jit(solution)/shard_map/brjpq,jqc->brpc/dot_general | solution.py:26
  50.0 1.2 fusion.13
  51.2 1.5 copy.64
  52.7 0.0 all-reduce.3.cloned.1.call-update
  52.7 0.0 all-gather.2.cloned.1.call-start
  52.8 71.3 %all-reduce.3.cloned.1.call-done = (bf16[4,4,4,128,128]{4,3,2,1,0:T(8,128)(2,1)}, bf16[4,4,128,256]{2,3,1,0:T(8,128)(2,1)}) async-done(((bf16[4,4,4,128,128]{4,3,2,1,0:T(8,128)(2,1)}, bf16[4,4,128,256]{2,3,1,0:T(8,128)(2,1)}), (bf16[4,4,4,128,128]{4,3,2,1,0:T(8,128)(2,1)}, bf16[4,4,128,256]{2,3,1,0:T(8,128)(2,1)})) %all-reduce.3.cloned.1.call-update) | async-done | bytes 3145744 | tf_op jit(solution)/shard_map/psum | solution.py:49
  124.1 1.5 collective-permute-start.1
  125.5 0.6 collective-permute-start
  126.1 46.8 %collective-permute-done.1 = bf16[4,4,4,128,128]{4,3,2,1,0:T(8,128)(2,1)} collective-permute-done((bf16[4,4,4,128,128]{4,3,2,1,0:T(8,128)(2,1)}, bf16[4,4,4,128,128]{4,3,2,1,0:T(8,128)(2,1)}, u32[]{:S(2)}, u32[]{:S(2)}) %collective-permute-start.1) | collective-permute-done | bytes 2097184 | tf_op jit(solution)/shard_map/ppermute | solution.py:12
  172.9 5.0 %fusion.11 = f32[4,128,128,4,4]{2,1,4,3,0:T(8,128)} fusion(bf16[4,4,4,128,128]{4,3,2,1,0:T(8,128)(2,1)} %collective-permute-done.1, bf16[4,4,4,128,128]{4,3,2,1,0:T(8,128)(2,1)} %get-tuple-element.5), kind=kLoop, calls=%fused_computation.16 | loop fusion | flops 3145728 | bytes 8388608 | tf_op jit(solution)/shard_map/jit(diagonal)/transpose | solution.py:56
  177.9 2.8 %gather_fusion = f32[4,4,128,128]{3,2,1,0:T(8,128)S(1)} fusion(f32[4,128,128,4,4]{2,1,4,3,0:T(8,128)} %fusion.11, s32[4]{0:T(128)S(1)} %or_bitcast_fusion.1), kind=kCustom, calls=%fused_computation | custom fusion | bytes 2097184 | tf_op jit(solution)/shard_map/jit(diagonal)/gather | solution.py:56
  180.7 16.5 %copy.67 = f32[4,4,128,128]{1,0,3,2:T(4,128)} copy(f32[4,4,128,128]{3,2,0,1:T(8,128)S(1)} %bitcast.91) | data formatting | bytes 2097152 | tf_op jit(solution)/shard_map/jit(diagonal)/transpose | solution.py:56
  197.2 1.9 gather_fusion.1
  199.1 0.1 copy.68
  199.2 0.0 copy-start.4
  199.2 0.0 copy-start.6
  199.2 0.0 collective-permute-done
  199.2 7.1 %fusion.24 = f32[4,4,128,64]{2,3,1,0:T(8,128)S(1)} fusion(bf16[4,4,4,128,128]{4,3,2,1,0:T(8,128)(2,1)} %collective-permute-done.1, bf16[4,4,4,128,128]{4,3,2,1,0:T(8,128)(2,1)} %get-tuple-element.5, f32[4,4,128]{2,1,0:T(4,128)S(1)} %copy.68, bf16[4,4,128,256]{2,3,1,0:T(8,128)(2,1)} %collective-permute-done, s32[]{:T(128)S(6)} %select_n.11, ...), kind=kOutput, calls=%fused_computation.29 | convolution fusion | flops 809893888 | bytes 5784576 | tf_op jit(solution)/shard_map/bklpq,blqc->bkpc/dot_general | solution.py:62
  206.4 0.0 copy-done.4
  206.4 0.0 copy-done.6
  206.4 6.1 %fusion.26 = f32[4,4,128,64]{2,3,1,0:T(8,128)S(1)} fusion(f32[4,4,128,64]{2,3,1,0:T(8,128)S(1)} %fusion.24, bf16[4,4,4,128,128]{4,3,2,1,0:T(8,128)(2,1)} %collective-permute-done.1, bf16[4,4,4,128,128]{4,3,2,1,0:T(8,128)(2,1)S(1)} %copy-done.4, f32[4,4,128]{2,1,0:T(4,128)S(1)} %copy.68, bf16[4,4,128,256]{2,3,1,0:T(8,128)(2,1)} %collective-permute-done, ...), kind=kOutput, calls=%fused_computation.31 | convolution fusion | flops 809238528 | bytes 6299652 | tf_op jit(solution)/shard_map/bklpq,blqc->bkpc/dot_general | solution.py:62
  212.5 6.1 %fusion.29 = bf16[4,4,128,64]{2,3,1,0:T(8,128)(2,1)S(1)} fusion(f32[4,4,128,64]{2,3,1,0:T(8,128)S(1)} %fusion.26, bf16[4,4,4,128,128]{4,3,2,1,0:T(8,128)(2,1)} %collective-permute-done.1, bf16[4,4,4,128,128]{4,3,2,1,0:T(8,128)(2,1)S(1)} %copy-done.4, f32[4,4,128]{2,1,0:T(4,128)S(1)} %copy.68, bf16[4,4,128,256]{2,3,1,0:T(8,128)(2,1)} %collective-permute-done, ...), kind=kOutput, calls=%fused_computation.34 | convolution fusion | flops 809369600 | bytes 6037508 | tf_op jit(solution)/shard_map/bklpq,blqc->bkpc/dot_general | solution.py:62
  218.6 0.9 copy.69
  219.5 0.0 all-gather.2.cloned.1.call-update
  219.5 16.9 %all-gather.2.cloned.1.call-done = bf16[4,4,128,256]{2,1,0,3:T(4,128)(2,1)} async-done(((bf16[4,4,128,64]{2,1,0,3:T(4,128)(2,1)}), bf16[4,4,128,256]{2,1,0,3:T(4,128)(2,1)}) %all-gather.2.cloned.1.call-update) | async-done | bytes 1048592 | tf_op jit(solution)/shard_map/all_gather | solution.py:64
  236.5 0.0 copy-start.1
  236.5 4.5 %fusion.12 = bf16[4,6,128,256]{3,2,1,0:T(8,128)(2,1)} fusion(bf16[4,6,128,256]{3,2,1,0:T(8,128)(2,1)S(1)} %bitcast_convert_fusion, bf16[4,6,4,128,128]{4,3,2,1,0:T(8,128)(2,1)} %copy-done.3, bf16[4,4,128,256,1]{2,1,0,3,4:T(4,128)(2,1)} %bitcast.93), kind=kOutput, calls=%fused_computation.18 | convolution fusion | flops 807665664 | bytes 7340032 | tf_op jit(solution)/shard_map/brkpq,bkqc->brpc/dot_general | solution.py:67
  240.9 0.0 copy-done.1
  (5 shorter events, 0.0 us)
Async XLA Ops:
  6.5 36.0 %copy-start = (bf16[3072,256]{1,0:T(8,128)(2,1)S(1)}, bf16[3072,256]{1,0:T(8,128)(2,1)}, u32[]{:S(2)}) copy-start(bf16[3072,256]{1,0:T(8,128)(2,1)} %param.7) | copy-start | bytes 4718596
  6.5 117.5 %all-reduce.3.cloned.1.call-start = ((), (), s32[]{:S(2)}) async-start(), calls=%async_computation.1 | async-start | bytes 6291456 | tf_op jit(solution)/shard_map/psum | solution.py:49
  9.2 29.1 %copy-start.5 = (s32[4,4]{1,0:T(4,128)S(1)}, s32[4,4]{1,0:T(4,128)}, u32[]{:S(2)}) copy-start(s32[4,4]{1,0:T(4,128)} %param.6) | copy-start | bytes 196
  34.5 10.1 %copy-start.2 = (bf16[4,6,24,128,128]{4,3,2,1,0:T(8,128)(2,1)S(1)}, bf16[4,6,24,128,128]{4,3,2,1,0:T(8,128)(2,1)}, u32[]{:S(2)}) copy-start(bf16[4,6,24,128,128]{4,3,2,1,0:T(8,128)(2,1)} %param.4) | copy-start | bytes 56623108
  38.3 2.3 copy-start.3
  52.7 183.8 %all-gather.2.cloned.1.call-start = ((), (), s32[]{:S(2)}) async-start(), calls=%async_computation | async-start | bytes 1310720 | tf_op jit(solution)/shard_map/all_gather | solution.py:64
  124.1 48.8 %collective-permute-start.1 = (bf16[4,4,4,128,128]{4,3,2,1,0:T(8,128)(2,1)}, bf16[4,4,4,128,128]{4,3,2,1,0:T(8,128)(2,1)}, u32[]{:S(2)}, u32[]{:S(2)}) collective-permute-start(bf16[4,4,4,128,128]{4,3,2,1,0:T(8,128)(2,1)} %get-tuple-element.5), channel_id=1, source_target_pairs={{0,4},{4,0},{8,12},{12,8},{16,20},{20,16},{24,28},{28,24},{1,5},{5... | collective-permute-start | bytes 6291464 | tf_op jit(solution)/shard_map/ppermute | solution.py:12
  125.5 73.7 %collective-permute-start = (bf16[4,4,128,256]{2,3,1,0:T(8,128)(2,1)}, bf16[4,4,128,256]{2,3,1,0:T(8,128)(2,1)}, u32[]{:S(2)}, u32[]{:S(2)}) collective-permute-start(bf16[4,4,128,256]{2,3,1,0:T(8,128)(2,1)} %get-tuple-element.6), channel_id=1, source_target_pairs={{0,4},{4,0},{8,12},{12,8},{16,20},{20,16},{24,28},{28,24},{1,5},{5... | collective-permute-start | bytes 3145736 | tf_op jit(solution)/shard_map/ppermute | solution.py:12
  199.2 7.2 %copy-start.4 = (bf16[4,4,4,128,128]{4,3,2,1,0:T(8,128)(2,1)S(1)}, bf16[4,4,4,128,128]{4,3,2,1,0:T(8,128)(2,1)}, u32[]{:S(2)}) copy-start(bf16[4,4,4,128,128]{4,3,2,1,0:T(8,128)(2,1)} %get-tuple-element.5) | copy-start | bytes 6291460
  199.2 7.2 %copy-start.6 = (bf16[4,4,128,256]{2,3,1,0:T(8,128)(2,1)S(1)}, bf16[4,4,128,256]{2,3,1,0:T(8,128)(2,1)}, u32[]{:S(2)}) copy-start(bf16[4,4,128,256]{2,3,1,0:T(8,128)(2,1)} %get-tuple-element.6) | copy-start | bytes 3145732
  236.5 4.5 %copy-start.1 = (bf16[3072,256]{1,0:T(8,128)(2,1)S(1)}, bf16[3072,256]{1,0:T(8,128)(2,1)}, u32[]{:S(2)}) copy-start(bf16[3072,256]{1,0:T(8,128)(2,1)} %param.7) | copy-start | bytes 4718596
Sparse Core Ops, SparseCore 0:
  52.8 71.1 all-reduce.2
  219.7 16.7 all-gather.1
where the time goes:
time: 248 us
  waiting for transfers between devices  135 us (54%)
  matrix products  58.9 us (24%)
  local copies, waits for them, and re-layouts  27.7 us (11%)
  between operations  13.5 us (5%)
  other arithmetic  10.5 us (4%)
    psum x1, waiting for transfers between devices, local(): lax.psum(slot_side.astype(jnp.bfloat16), 'face').astype(jnp.float32)  71.3 us
    ppermute x2, waiting for transfers between devices, partner(): return lax.ppermute(value, axis, pairs)  46.8 us
    dot_general x1, matrix products, local(): jnp.einsum('brjpq,bkj->brkpq', blocks, column_pick, preferred_element_typ...  25.3 us
    dot_general x3, matrix products, local(): jnp.einsum('bklpq,blqc->bkpc', system, potential, precision=lax.Precision...  19.4 us
    all_gather x1, waiting for transfers between devices, local(): lax.all_gather(potential.astype(jnp.bfloat16), 'face', axis=3, tiled=True)  16.9 us
    transpose x1, local copies, waits for them, and re-layouts, local(): jnp.diagonal(jnp.diagonal(system, axis1=1, axis2=2), axis1=1, axis2=2)  16.5 us
    dot_general x1, matrix products, local(): jnp.einsum('brjpq,jqc->brpc', kept_ext, sketch_blocks, preferred_element_...  5.47 us
    transpose x1, other arithmetic, local(): jnp.diagonal(system, axis1=1, axis2=2)  4.99 us
  transfers between devices with their start and end apart: 4, of which 3 were waited for; matrix products, arithmetic and copies ran while one was open for 11% of the time, Pallas kernels for 0%

commit v1 on v0

--- a/solution.py
+++ b/solution.py
@@ -4,6 +4,7 @@
 from jax.sharding import PartitionSpec as P
 
 ITERS = 4
+leaves_save = lambda u_in, comm_axis: lax.all_gather(u_in, comm_axis).sum(axis=0)
 
 
 def partner(value, axis, stride):
@@ -46,7 +47,7 @@
     )
     here_y, here_side = (
         lax.psum(slot_y.astype(jnp.bfloat16), "face").astype(jnp.float32),
-        lax.psum(slot_side.astype(jnp.bfloat16), "face").astype(jnp.float32),
+        leaves_save(slot_side.astype(jnp.bfloat16), "face").astype(jnp.float32),
     )
     there_y, there_side = partner(
         (here_y.astype(jnp.bfloat16), here_side.astype(jnp.bfloat16)), "box", 0

time: 248 us -> 233 us (0.940)
  waiting for transfers between devices: 135 us -> 113 us
  other arithmetic: 10.5 us -> 17.6 us
    all_gather x0 -> x1, waiting for transfers between devices: none -> 60.9 us  [lax.all_gather(u_in, comm_axis).sum(axis=0)]
    ppermute x2, waiting for transfers between devices: 46.8 us -> 0.02 us  [partner(): return lax.ppermute(value, axis, pairs)]
    psum x1, waiting for transfers between devices: 71.3 us -> 35.7 us  [local(): lax.psum(slot_y.astype(jnp.bfloat16), 'face').astype(jnp.float32)]
    reduce_sum x0 -> x1, other arithmetic: none -> 7.26 us  [lax.all_gather(u_in, comm_axis).sum(axis=0)]
    dot_general x1, matrix products: 5.47 us -> 9.1 us  [local(): jnp.einsum('brjpq,jqc->brpc', kept_ext, sketch_blocks, preferred_element_...]
  transfers between devices with their start and end apart: 4 -> 5, of which waited for: 3 -> 3; matrix products, arithmetic and copies ran while one was open for 11% -> 16% of each run, Pallas kernels for 0% -> 0%
where the time goes in v1:
time: 233 us
  waiting for transfers between devices  113 us (48%)
  matrix products  60.2 us (26%)
  local copies, waits for them, and re-layouts  25.7 us (11%)
  other arithmetic  17.6 us (8%)
  between operations  13.2 us (6%)
  starting transfers between devices  3.21 us (1%)
    all_gather x1, waiting for transfers between devices, lax.all_gather(u_in, comm_axis).sum(axis=0)  60.9 us
    psum x1, waiting for transfers between devices, local(): lax.psum(slot_y.astype(jnp.bfloat16), 'face').astype(jnp.float32)  35.7 us
    dot_general x1, matrix products, local(): jnp.einsum('brjpq,bkj->brkpq', blocks, column_pick, preferred_element_typ...  23 us
    dot_general x3, matrix products, local(): jnp.einsum('bklpq,blqc->bkpc', system, potential, precision=lax.Precision...  19.4 us
    transpose x1, local copies, waits for them, and re-layouts, local(): jnp.diagonal(jnp.diagonal(system, axis1=1, axis2=2), axis1=1, axis2=2)  16.5 us
    all_gather x1, waiting for transfers between devices, local(): lax.all_gather(potential.astype(jnp.bfloat16), 'face', axis=3, tiled=True)  16.1 us
    dot_general x1, matrix products, local(): jnp.einsum('brjpq,jqc->brpc', kept_ext, sketch_blocks, preferred_element_...  9.1 us
    reduce_sum x1, other arithmetic, lax.all_gather(u_in, comm_axis).sum(axis=0)  7.26 us
  transfers between devices with their start and end apart: 5, of which 3 were waited for; matrix products, arithmetic and copies ran while one was open for 16% of the time, Pallas kernels for 0%

profile of v1, /device:TPU:0, one launch (start us, length us, event | category | flops | bytes accessed | tf_op | source)
XLA Modules:
  0.0 232.8 jit_solution(10451698992959360161)
XLA Ops:
  6.5 0.0 copy-start
  6.5 0.0 all-gather.6.cloned.1.call-start
  6.5 0.9 fusion.43
  7.4 0.8 fusion.52
  8.2 0.9 convolution_bitcast_fusion
  9.1 0.1 copy.71
  9.2 23.0 %fusion = f32[4,4,6,128,128]{4,1,3,2,0:T(4,128)} fusion(bf16[4,6,24,128,128]{4,3,2,1,0:T(8,128)(2,1)} %param.4, s32[4,4]{1,0:T(4,128)} %param.6), kind=kOutput, calls=%fused_computation.2 | convolution fusion | flops 75497856 | bytes 25165888 | tf_op jit(solution)/shard_map/brjpq,bkj->brkpq/dot_general | solution.py:31
  32.2 0.0 copy-start.4
  32.2 3.6 %fusion.5 = bf16[4,6,4,128,128]{4,3,2,1,0:T(8,128)(2,1)S(1)} fusion(f32[4,4,6,128,128]{4,1,3,2,0:T(4,128)} %fusion, f32[4,6,4]{2,1,0:T(8,128)S(1)} %copy.71), kind=kLoop, calls=%fused_computation.8 | loop fusion | flops 3145728 | bytes 9437568 | tf_op jit(solution)/shard_map/convert_element_type | solution.py:40
  35.8 0.0 copy-done.4
  35.8 0.0 copy-start.2
  35.8 2.3 fusion.15
  38.1 0.0 copy-done.2
  38.1 1.9 copy.75
  40.0 0.0 all-gather.6.cloned.1.call-update
  40.1 0.2 all-reduce.2.cloned.1.call-start
  40.3 60.9 %all-gather.6.cloned.1.call-done = bf16[16,4,4,128,128]{4,3,2,1,0:T(8,128)(2,1)} async-done(((bf16[4,4,4,128,128]{4,3,2,1,0:T(8,128)(2,1)}), bf16[16,4,4,128,128]{4,3,2,1,0:T(8,128)(2,1)}) %all-gather.6.cloned.1.call-update) | async-done | bytes 8388624 | tf_op jit(solution)/shard_map/all_gather | solution.py:7
  101.2 7.3 %reduce_sum.12 = bf16[4,4,4,128,128]{4,3,2,1,0:T(8,128)(2,1)} reduce(bf16[4,4,4,4,128,128]{5,4,3,2,1,0:T(8,128)(2,1)} %bitcast.93, bf16[]{:T(256)} %constant.28.clone.1), dimensions={0}, to_apply=%region_2.0 | reduce | flops 3145728 | bytes 10485762 | tf_op jit(solution)/shard_map/reduce_sum | solution.py:7
  108.5 1.5 collective-permute-start.1
  109.9 0.0 copy-done
  109.9 9.1 %bitcast_convert_fusion = bf16[4,6,128,256]{3,2,1,0:T(8,128)(2,1)S(1)} fusion(bf16[24,128,256,1,1]{2,1,0,4,3:T(8,128)(2,1)S(1)} %bitcast.91, bf16[4,6,24,128,128]{4,3,2,1,0:T(8,128)(2,1)} %param.4, bf16[4,6,24]{2,1,0:T(8,128)(2,1)S(1)} %copy.67), kind=kOutput, calls=%fused_computation.18 | convolution fusion | flops 4842061824 | bytes 22021248 | tf_op jit(solution)/shard_map/brjpq,jqc->brpc/dot_general | solution.py:27
  119.0 1.2 fusion.13
  120.2 1.5 copy.73
  121.7 0.0 all-reduce.2.cloned.1.call-update
  121.7 0.0 all-gather.4.cloned.1.call-start
  121.8 35.7 %all-reduce.2.cloned.1.call-done = bf16[4,4,128,256]{2,3,1,0:T(8,128)(2,1)} async-done(((bf16[4,4,128,256]{2,3,1,0:T(8,128)(2,1)}), bf16[4,4,128,256]{2,3,1,0:T(8,128)(2,1)}) %all-reduce.2.cloned.1.call-update) | async-done | bytes 1048592 | tf_op jit(solution)/shard_map/psum | solution.py:49
  157.5 1.5 collective-permute-start
  159.0 0.0 collective-permute-done.1
  159.0 5.0 %fusion.11 = f32[4,128,128,4,4]{2,1,4,3,0:T(8,128)} fusion(bf16[4,4,4,128,128]{4,3,2,1,0:T(8,128)(2,1)} %collective-permute-done.1, bf16[4,4,4,128,128]{4,3,2,1,0:T(8,128)(2,1)} %reduce_sum.12), kind=kLoop, calls=%fused_computation.15 | loop fusion | flops 3145728 | bytes 8388608 | tf_op jit(solution)/shard_map/jit(diagonal)/transpose | solution.py:57
  164.0 2.8 %gather_fusion = f32[4,4,128,128]{3,2,1,0:T(8,128)S(1)} fusion(f32[4,128,128,4,4]{2,1,4,3,0:T(8,128)} %fusion.11, s32[4]{0:T(128)S(1)} %or_bitcast_fusion.1), kind=kCustom, calls=%fused_computation | custom fusion | bytes 2097184 | tf_op jit(solution)/shard_map/jit(diagonal)/gather | solution.py:57
  166.8 16.5 %copy.79 = f32[4,4,128,128]{1,0,3,2:T(4,128)} copy(f32[4,4,128,128]{3,2,0,1:T(8,128)S(1)} %bitcast.92) | data formatting | bytes 2097152 | tf_op jit(solution)/shard_map/jit(diagonal)/transpose | solution.py:57
  183.3 1.9 gather_fusion.1
  185.2 0.1 copy.80
  185.3 0.0 copy-start.3
  185.3 0.0 copy-start.5
  185.3 0.0 collective-permute-done
  185.4 7.1 %fusion.27 = f32[4,4,128,64]{2,3,1,0:T(8,128)S(1)} fusion(bf16[4,4,4,128,128]{4,3,2,1,0:T(8,128)(2,1)} %collective-permute-done.1, bf16[4,4,4,128,128]{4,3,2,1,0:T(8,128)(2,1)} %reduce_sum.12, f32[4,4,128]{2,1,0:T(4,128)S(1)} %copy.80, bf16[4,4,128,256]{2,3,1,0:T(8,128)(2,1)} %collective-permute-done, s32[]{:T(128)S(6)} %select_n.11, ...), kind=kOutput, calls=%fused_computation.29 | convolution fusion | flops 809893888 | bytes 5784576 | tf_op jit(solution)/shard_map/bklpq,blqc->bkpc/dot_general | solution.py:63
  192.5 0.0 copy-done.3
  192.5 0.0 copy-done.5
  192.5 6.1 %fusion.29 = f32[4,4,128,64]{2,3,1,0:T(8,128)S(1)} fusion(f32[4,4,128,64]{2,3,1,0:T(8,128)S(1)} %fusion.27, bf16[4,4,4,128,128]{4,3,2,1,0:T(8,128)(2,1)} %collective-permute-done.1, bf16[4,4,4,128,128]{4,3,2,1,0:T(8,128)(2,1)S(1)} %copy-done.3, f32[4,4,128]{2,1,0:T(4,128)S(1)} %copy.80, bf16[4,4,128,256]{2,3,1,0:T(8,128)(2,1)} %collective-permute-done, ...), kind=kOutput, calls=%fused_computation.31 | convolution fusion | flops 809238528 | bytes 6299652 | tf_op jit(solution)/shard_map/bklpq,blqc->bkpc/dot_general | solution.py:63
  198.6 6.1 %fusion.32 = bf16[4,4,128,64]{2,3,1,0:T(8,128)(2,1)S(1)} fusion(f32[4,4,128,64]{2,3,1,0:T(8,128)S(1)} %fusion.29, bf16[4,4,4,128,128]{4,3,2,1,0:T(8,128)(2,1)} %collective-permute-done.1, bf16[4,4,4,128,128]{4,3,2,1,0:T(8,128)(2,1)S(1)} %copy-done.3, f32[4,4,128]{2,1,0:T(4,128)S(1)} %copy.80, bf16[4,4,128,256]{2,3,1,0:T(8,128)(2,1)} %collective-permute-done, ...), kind=kOutput, calls=%fused_computation.34 | convolution fusion | flops 809369600 | bytes 6037508 | tf_op jit(solution)/shard_map/bklpq,blqc->bkpc/dot_general | solution.py:63
  204.8 0.9 copy.81
  205.7 0.0 all-gather.4.cloned.1.call-update
  205.7 16.1 %all-gather.4.cloned.1.call-done = bf16[4,4,128,256]{2,1,0,3:T(4,128)(2,1)} async-done(((bf16[4,4,128,64]{2,1,0,3:T(4,128)(2,1)}), bf16[4,4,128,256]{2,1,0,3:T(4,128)(2,1)}) %all-gather.4.cloned.1.call-update) | async-done | bytes 1048592 | tf_op jit(solution)/shard_map/all_gather | solution.py:65
  221.8 0.0 copy-start.1
  221.8 4.5 %fusion.12 = bf16[4,6,128,256]{3,2,1,0:T(8,128)(2,1)} fusion(bf16[4,6,128,256]{3,2,1,0:T(8,128)(2,1)S(1)} %bitcast_convert_fusion, bf16[4,6,4,128,128]{4,3,2,1,0:T(8,128)(2,1)} %copy-done.2, bf16[4,4,128,256,1]{2,1,0,3,4:T(4,128)(2,1)} %bitcast.95), kind=kOutput, calls=%fused_computation.17 | convolution fusion | flops 807665664 | bytes 7340032 | tf_op jit(solution)/shard_map/brkpq,bkqc->brpc/dot_general | solution.py:68
  226.3 0.0 copy-done.1
  (5 shorter events, 0.0 us)
Async XLA Ops:
  6.5 103.4 %copy-start = (bf16[3072,256]{1,0:T(8,128)(2,1)S(1)}, bf16[3072,256]{1,0:T(8,128)(2,1)}, u32[]{:S(2)}) copy-start(bf16[3072,256]{1,0:T(8,128)(2,1)} %param.7) | copy-start | bytes 4718596
  6.5 94.7 %all-gather.6.cloned.1.call-start = ((), (), s32[]{:S(2)}) async-start(), calls=%async_computation.2 | async-start | bytes 10485760 | tf_op jit(solution)/shard_map/all_gather | solution.py:7
  32.2 3.7 %copy-start.4 = (s32[4,4]{1,0:T(4,128)S(1)}, s32[4,4]{1,0:T(4,128)}, u32[]{:S(2)}) copy-start(s32[4,4]{1,0:T(4,128)} %param.6) | copy-start | bytes 196
  35.8 2.3 copy-start.2
  40.1 117.5 %all-reduce.2.cloned.1.call-start = ((), (), s32[]{:S(2)}) async-start(), calls=%async_computation | async-start | bytes 2097152 | tf_op jit(solution)/shard_map/psum | solution.py:49
  108.5 50.6 %collective-permute-start.1 = (bf16[4,4,4,128,128]{4,3,2,1,0:T(8,128)(2,1)}, bf16[4,4,4,128,128]{4,3,2,1,0:T(8,128)(2,1)}, u32[]{:S(2)}, u32[]{:S(2)}) collective-permute-start(bf16[4,4,4,128,128]{4,3,2,1,0:T(8,128)(2,1)} %reduce_sum.12), channel_id=1, source_target_pairs={{0,4},{4,0},{8,12},{12,8},{16,20},{20,16},{24,28},{28,24},{1,5},{5... | collective-permute-start | bytes 6291464 | tf_op jit(solution)/shard_map/ppermute | solution.py:13
  121.7 100.1 %all-gather.4.cloned.1.call-start = ((), (), s32[]{:S(2)}) async-start(), calls=%async_computation.1 | async-start | bytes 1310720 | tf_op jit(solution)/shard_map/all_gather | solution.py:65
  157.5 27.8 %collective-permute-start = (bf16[4,4,128,256]{2,3,1,0:T(8,128)(2,1)}, bf16[4,4,128,256]{2,3,1,0:T(8,128)(2,1)}, u32[]{:S(2)}, u32[]{:S(2)}) collective-permute-start(bf16[4,4,128,256]{2,3,1,0:T(8,128)(2,1)} %all-reduce.2.cloned.1.call-done), channel_id=1, source_target_pairs={{0,4},{4,0},{8,12},{12,8},{16,20},{20,16},{24,28},{28,24},{1,5},{5... | collective-permute-start | bytes 3145736 | tf_op jit(solution)/shard_map/ppermute | solution.py:13
  185.3 7.2 %copy-start.3 = (bf16[4,4,4,128,128]{4,3,2,1,0:T(8,128)(2,1)S(1)}, bf16[4,4,4,128,128]{4,3,2,1,0:T(8,128)(2,1)}, u32[]{:S(2)}) copy-start(bf16[4,4,4,128,128]{4,3,2,1,0:T(8,128)(2,1)} %reduce_sum.12) | copy-start | bytes 6291460
  185.3 7.2 %copy-start.5 = (bf16[4,4,128,256]{2,3,1,0:T(8,128)(2,1)S(1)}, bf16[4,4,128,256]{2,3,1,0:T(8,128)(2,1)}, u32[]{:S(2)}) copy-start(bf16[4,4,128,256]{2,3,1,0:T(8,128)(2,1)} %all-reduce.2.cloned.1.call-done) | copy-start | bytes 3145732
  221.8 4.5 %copy-start.1 = (bf16[3072,256]{1,0:T(8,128)(2,1)S(1)}, bf16[3072,256]{1,0:T(8,128)(2,1)}, u32[]{:S(2)}) copy-start(bf16[3072,256]{1,0:T(8,128)(2,1)} %param.7) | copy-start | bytes 4718596
Sparse Core Ops, SparseCore 0:
  40.2 60.9 all-gather.5
  121.8 35.6 all-reduce.1
  205.8 15.9 all-gather.3
